TPU v7x, 256 devices: a whole 4x4x8 slice. The times are simulated.
256 devices in a mesh: space: 32 (over y, z), chan: 8 (over x, core).
Axes of the slice: x: 4, y: 4, z: 8, core: 2. Of those that a mesh axis runs over, the one named last changes fastest.
Arguments:
- features: bfloat16 [65536, 256], P('space', 'chan'), may hold values from -6 to 6
- kernel_map: int32 [32, 27, 16, 3], P('space'), may hold values from 0 to 31, as said below
- block_count: int32 [32], replicated, may hold values from 3 to 16, as said below
- weight_one: bfloat16 [27, 256, 256], P(None, 'chan'), may hold values from -0.078125 to 0.078125
- weight_two: bfloat16 [27, 256, 256], P(None, 'chan'), may hold values from -0.078125 to 0.078125
- cotangent: bfloat16 [65536, 256], P('space', 'chan'), may hold values from -0.026977539 to 0.026977539
Outputs:
- output: bfloat16 [65536, 256], P('space', 'chan')
- grad_one: float32 [27, 256, 256], P(None, 'chan', 'space')
- grad_two: float32 [27, 256, 256], P(None, 'chan', 'space')
Inputs may be any that keep to these rules, and one draw needn't show every extreme that they name: `kernel_map`: column 0 of slab s's entries is s - 1, s or s + 1. Column 1 is a block below block_count of that source slab; from slab s - 1 it is one of that slab's last 2 live blocks, from slab s + 1 one of its first 2. Column 2 lies below 16. Entries stand in offset order, 16 per offset and slab. `block_count`: at least one slab has all 16 blocks live.
All inputs are finite; a program needn't handle non-finite values.
Results may differ from a plain program's by a relative error of at most 0.015.
Values may be sent and summed in bfloat16 or wider, within the bound.
A program may use at most 64 MiB of HBM per device.

v0:
```python
import jax
import jax.numpy as jnp
from jax import lax
from jax.sharding import PartitionSpec as P

BLK = 128
HB = 2


def padded(shard, sides, width):
    for axis, dim in sides:
        size, length = (lax.axis_size(axis), shard.shape[dim])
        up = [(i, (i + 1) % size) for i in range(size - 1)]
        down = [(j, i) for i, j in up]
        last = lax.slice_in_dim(shard, length - width, length, axis=dim)
        leading = lax.slice_in_dim(shard, 0, width, axis=dim)
        before = lax.ppermute(last, axis, up)
        after = lax.ppermute(leading, axis, down)
        shard = jnp.concatenate([before, shard, after], axis=dim)
    return shard


def local(features, kernel_map, block_count, weight_one, weight_two, cotangent):
    shard = lax.axis_index("space")
    nblocks = features.shape[0] // BLK
    own_count = block_count[shard]
    left_count = block_count[jnp.maximum(shard - 1, 0)]
    entries = kernel_map[0]
    source = entries[..., 0]
    inblock = entries[..., 1]
    target = entries[..., 2]
    position = jnp.where(
        source == shard,
        HB + inblock,
        jnp.where(source < shard, inblock - (left_count - HB), HB + nblocks + inblock),
    )
    live = target < own_count
    select = (target[..., None] == jnp.arange(nblocks, dtype=jnp.int32)) & live[..., None]
    select_f = select.astype(jnp.float32)
    select_b = select.astype(jnp.bfloat16)
    place = (
        (position[..., None] == jnp.arange(nblocks + 2 * HB, dtype=jnp.int32)) & live[..., None]
    ).astype(jnp.float32)

    def widen(feat):
        return lax.all_gather(feat, "chan", axis=1, tiled=True)

    def attach_rims(feat):
        width = feat.shape[1]
        cube = feat.reshape(nblocks, BLK, width)
        first = cube[:HB]
        last = lax.dynamic_slice_in_dim(cube, own_count - HB, HB, 0)
        rims = jnp.concatenate([first, last], 0).reshape(2 * HB * BLK, width)
        outer = padded(rims, (("space", 0),), HB * BLK)
        return jnp.concatenate([outer[: HB * BLK], feat, outer[3 * HB * BLK :]], 0)

    def extend(feat):
        return attach_rims(widen(feat))

    def convolve(wide, weights):
        cube = wide.reshape(-1, BLK, wide.shape[1])

        def convolve_add_offset(total, item):
            index, choose, kernel = item
            picked = cube[index]
            prod = jnp.einsum("erc,dc->erd", picked, kernel, preferred_element_type=jnp.float32)
            return (total + jnp.einsum("eb,erd->brd", choose, prod), None)

        start = jnp.zeros((nblocks, BLK, weights.shape[1]), jnp.float32)
        total, _ = lax.scan(convolve_add_offset, start, (position, select_f, weights))
        return total.reshape(nblocks * BLK, weights.shape[1])

    def weight_grad(wide, grads_cube):
        cube = wide.reshape(-1, BLK, wide.shape[1])

        def one_offset(item):
            index, choose = item
            picked = cube[index]
            chosen = jnp.einsum(
                "eb,brd->erd", choose, grads_cube, preferred_element_type=jnp.float32
            ).astype(jnp.bfloat16)
            return jnp.einsum("erc,erd->dc", picked, chosen, preferred_element_type=jnp.float32)

        return lax.map(one_offset, (position, select_b))

    wide_x = extend(features)
    z_one = convolve(wide_x, weight_one)
    hidden = jax.nn.silu(z_one).astype(jnp.bfloat16)
    wide_h = extend(hidden)
    output = convolve(wide_h, weight_two).astype(jnp.bfloat16)
    grad_cube = cotangent.reshape(nblocks, BLK, -1)
    grad_two = weight_grad(wide_h, grad_cube)
    width = cotangent.shape[1]

    def spread_add_offset(total, item):
        choose, spot, kernel = item
        chosen = jnp.einsum(
            "eb,brd->erd", choose, grad_cube, preferred_element_type=jnp.float32
        ).astype(jnp.bfloat16)
        contrib = jnp.einsum("erd,dc->erc", chosen, kernel, preferred_element_type=jnp.float32)
        return (total + jnp.einsum("ex,erc->xrc", spot, contrib), None)

    start = jnp.zeros((nblocks + 2 * HB, BLK, weight_two.shape[2]), jnp.float32)
    total, _ = lax.scan(spread_add_offset, start, (select_b, place, weight_two))
    partial_value = total.reshape((nblocks + 2 * HB) * BLK, weight_two.shape[2])
    summed = lax.psum_scatter(partial_value, "chan", scatter_dimension=1, tiled=True)
    width = summed.shape[1]
    cube = summed.reshape(-1, BLK, width)
    edges = jnp.concatenate([cube[:HB], cube[HB + nblocks :]], 0).reshape(2 * HB * BLK, width)
    back = padded(edges, (("space", 0),), HB * BLK)
    inner = cube[HB : HB + nblocks]
    from_left = back[: HB * BLK].reshape(HB, BLK, width)
    from_right = back[3 * HB * BLK :].reshape(HB, BLK, width)
    inner = inner.at[:HB].add(from_left)
    tail = lax.dynamic_slice_in_dim(inner, own_count - HB, HB, 0) + from_right
    inner = lax.dynamic_update_slice_in_dim(inner, tail, own_count - HB, 0)
    grad_hidden = inner.reshape(nblocks * BLK, width)
    gate = jax.nn.sigmoid(z_one)
    grad_z = (grad_hidden * gate * (1.0 + z_one * (1.0 - gate))).astype(jnp.bfloat16)
    grad_one = weight_grad(wide_x, grad_z.reshape(nblocks, BLK, -1))
    totals = (
        lax.psum_scatter(grad_one, "space", scatter_dimension=2, tiled=True),
        lax.psum_scatter(grad_two, "space", scatter_dimension=2, tiled=True),
    )
    return (output, totals[0], totals[1])


def solution(mesh):
    return jax.shard_map(
        local,
        mesh=mesh,
        in_specs=(
            P("space", "chan"),
            P("space", None, None, None),
            P(),
            P(None, "chan", None),
            P(None, "chan", None),
            P("space", "chan"),
        ),
        out_specs=(P("space", "chan"), P(None, "chan", "space"), P(None, "chan", "space")),
        check_vma=False,
    )
```

profile of v0, /device:TPU:4, one launch (start us, length us, event | category | flops | bytes accessed | tf_op | source)
XLA Modules:
  0.0 890.1 jit_solution(15789710916156473926)
XLA Ops:
  14.6 22.7 %all-gather.3.cloned.1.call-done = bf16[2048,256]{0,1:T(8,128)(2,1)} async-done(((bf16[2048,32]{0,1:T(8,128)(2,1)}), bf16[2048,256]{0,1:T(8,128)(2,1)}) %all-gather.3.cloned.1.call-update) | async-done | bytes 1048592 | tf_op jit(solution)/shard_map/all_gather | solution.py:46
  39.1 3.5 collective-permute-start
  45.7 4.2 collective-permute-done.1
  53.5 173.4 %while.56 = (s32[]{:T(128)}, f32[16,128,32]{1,0,2:T(8,128)}, bf16[27,16,16]{1,2,0:T(8,128)(2,1)}, s32[27,16]{1,0:T(8,128)S(1)}, bf16[20,128,256]{2,1,0:T(8,128)(...) while((s32[]{:T(128)}, f32[16,128,32]{1,0,2:T(8,128)}, ...), condition=%wide.region_1.2_spmd.clone, body=%wide.region_0.1_spmd.clone.sunk | while | flops 35783728 | bytes 3958115 | solution.py:70
  53.5 2.9 gather_fusion.2
  59.6 2.9 gather_fusion.2
  66.1 2.9 gather_fusion.2
  72.5 2.9 gather_fusion.2
  78.9 2.9 gather_fusion.2
  85.4 2.9 gather_fusion.2
  91.8 2.9 gather_fusion.2
  98.2 2.9 gather_fusion.2
  104.7 2.9 gather_fusion.2
  111.1 2.9 gather_fusion.2
  117.5 2.9 gather_fusion.2
  124.0 2.9 gather_fusion.2
  130.4 2.9 gather_fusion.2
  136.8 2.9 gather_fusion.2
  143.3 2.9 gather_fusion.2
  149.7 2.9 gather_fusion.2
  156.1 2.9 gather_fusion.2
  162.6 2.9 gather_fusion.2
  169.0 2.9 gather_fusion.2
  175.4 2.9 gather_fusion.2
  181.9 2.9 gather_fusion.2
  188.3 2.9 gather_fusion.2
  194.8 2.9 gather_fusion.2
  201.2 2.9 gather_fusion.2
  207.6 2.9 gather_fusion.2
  214.1 2.9 gather_fusion.2
  220.5 2.9 gather_fusion.2
  228.7 108.4 %while.58 = (s32[]{:T(128)}, f32[20,128,256]{2,0,1:T(8,128)S(1)}, bf16[27,16,20]{2,1,0:T(8,128)(2,1)}, bf16[27,16,16]{2,1,0:T(8,128)(2,1)S(1)}, bf16[16,128,32]{...) while((s32[]{:T(128)}, f32[20,128,256]{2,0,1:T(8,128)S(1)}, ...), condition=%wide.region_5.6_spmd.clone, body=%wide.region_4.5_spmd.clone.sunk | while | flops 57999360 | bytes 6317155 | solution.py:104
  242.2 2.6 select_add_fusion.2
  246.2 2.6 select_add_fusion.2
  258.3 2.6 select_add_fusion.2
  266.3 2.6 select_add_fusion.2
  282.4 2.6 select_add_fusion.2
  339.5 3.2 copy.71
  344.4 3.5 collective-permute-start.2
  350.3 4.9 collective-permute-done.3
  355.3 21.4 %reduce-scatter.10.cloned.1.call-done = f32[32,2560]{1,0:T(8,128)} async-done(((f32[256,2560]{1,0:T(8,128)}), f32[32,2560]{1,0:T(8,128)}) %reduce-scatter.10.cloned.1.call-update) | async-done | bytes 327696
  378.3 4.1 collective-permute-start.4
  385.5 64.0 %while.55 = (s32[]{:T(128)}, f32[27,32,256]{2,1,0:T(8,128)}, bf16[27,16,16]{2,1,0:T(8,128)(2,1)S(1)}, bf16[16,128,32]{1,0,2:T(8,128)(2,1)S(1)}, s32[27,16]{1,0:T...) while((s32[]{:T(128)}, f32[27,32,256]{2,1,0:T(8,128)}, bf16[27,16,16]{2,1,0:T(8,128)(2,1)S(1)}, ...), condition=%wide.region_11.12_spmd, body=%wide.region_10.11_spmd.sunk | while | flops 35718192 | bytes 3580757 | solution.py:84
  449.5 3.4 copy.69
  462.4 141.8 %while.54 = (s32[]{:T(128)}, f32[27,32,256]{2,1,0:T(8,128)}, bf16[27,16,16]{2,1,0:T(8,128)(2,1)}, bf16[16,128,32]{1,0,2:T(8,128)(2,1)S(1)}, s32[27,16]{1,0:T(8,1...) while((s32[]{:T(128)}, f32[27,32,256]{2,1,0:T(8,128)}, bf16[27,16,16]{2,1,0:T(8,128)(2,1)}, ...), condition=%wide.region_8.9_spmd, body=%wide.region_7.8_spmd.sunk | while | flops 35718192 | bytes 3581265 | solution.py:84
  604.3 3.4 copy.68
  607.6 91.3 %while.57 = (s32[]{:T(128)}, f32[16,128,32]{1,0,2:T(8,128)S(1)}, bf16[27,16,16]{1,2,0:T(8,128)(2,1)}, s32[27,16]{1,0:T(8,128)}, bf16[20,128,256]{2,1,0:T(8,128)(...) while((s32[]{:T(128)}, f32[16,128,32]{1,0,2:T(8,128)S(1)}, ...), condition=%wide.region_3.4_spmd.clone, body=%wide.region_2.3_spmd.clone.sunk | while | flops 35783728 | bytes 3958115 | solution.py:70
  699.6 184.0 %reduce-scatter.6.cloned.1.call-done = f32[27,32,8]{1,2,0:T(8,128)} async-done(((f32[27,32,256]{1,2,0:T(8,128)}), f32[27,32,8]{1,2,0:T(8,128)}) %reduce-scatter.6.cloned.1.call-update) | async-done | bytes 27664 | tf_op jit(solution)/shard_map/reduce_scatter | solution.py:122
  (661 shorter events, 520.7 us)
Async XLA Ops:
  7.2 30.2 %all-gather.3.cloned.1.call-start = ((), (), s32[]{:S(2)}) async-start(), calls=%async_computation.3 | async-start | bytes 1179648 | tf_op jit(solution)/shard_map/all_gather | solution.py:46
  7.9 334.9 %all-gather.5.cloned.1.call-start = ((), (), s32[]{:S(2)}) async-start(), calls=%async_computation.4 | async-start | bytes 1179648 | tf_op jit(solution)/shard_map/all_gather | solution.py:46
  37.3 5.2 copy-start.2
  39.1 6.6 collective-permute-start
  42.6 7.2 collective-permute-start.1
  226.9 1.8 copy-start.5
  228.7 148.1 %reduce-scatter.10.cloned.1.call-start = ((), (), s32[]{:S(2)}) async-start(), calls=%async_computation.7 | async-start | bytes 2949120
  342.8 356.9 %reduce-scatter.8.cloned.1.call-start = ((), (), s32[]{:S(2)}) async-start(), calls=%async_computation.6 | async-start | bytes 3649536 | tf_op jit(solution)/shard_map/reduce_scatter | solution.py:123
  344.4 6.0 collective-permute-start.2
  347.8 7.4 collective-permute-start.3
  378.3 79.2 %collective-permute-start.4 = (f32[256,32]{1,0:T(8,128)}, f32[256,32]{1,0:T(8,128)}, u32[]{:S(2)}, u32[]{:S(2)}) collective-permute-start(f32[256,32]{1,0:T(8,128)} %copy.75), channel_id=1, source_target_pairs={{0,8},{8,16},{16,24},{24,32},{32,40},{40,48},{48,56},{56,64},{64,7... | collective-permute-start | bytes 98312 | tf_op jit(solution)/shard_map/ppermute | solution.py:17
  383.2 76.1 %collective-permute-start.5 = (f32[256,32]{1,0:T(8,128)}, f32[256,32]{1,0:T(8,128)}, u32[]{:S(2)}, u32[]{:S(2)}) collective-permute-start(f32[256,32]{1,0:T(8,128)} %copy.76), channel_id=1, source_target_pairs={{8,0},{16,8},{24,16},{32,24},{40,32},{48,40},{56,48},{64,56},{72,6... | collective-permute-start | bytes 98312 | tf_op jit(solution)/shard_map/ppermute | solution.py:18
  449.5 3.4 copy-start.3
  452.9 1.0 copy-start.4
  452.9 8.4 copy-start.1
  452.9 430.6 %reduce-scatter.6.cloned.1.call-start = ((), (), s32[]{:S(2)}) async-start(), calls=%async_computation.5 | async-start | bytes 3649536 | tf_op jit(solution)/shard_map/reduce_scatter | solution.py:122
  453.9 8.6 copy-start
Sparse Core Ops, SparseCore 0:
  9.9 27.4 all-gather.2
  228.8 25.9 all-gather.4
  342.9 33.8 reduce-scatter.9
  453.0 216.3 reduce-scatter.7
  674.3 209.1 reduce-scatter.5
where the time goes:
time: 900 us; the launch traced here: 890 us
  matrix products  331 us (37%)
  waiting for transfers between devices  240 us (27%)
  local copies, waits for them, and re-layouts  223 us (25%)
  other arithmetic  62.2 us (7%)
  between operations  16 us (2%)
  starting transfers between devices  15.1 us (2%)
    reduce_scatter x1, waiting for transfers between devices, local(): lax.psum_scatter(grad_one, 'space', scatter_dimension=2, tiled=True)  184 us
    gather x54, local copies, waits for them, and re-layouts, convolve_add_offset(): picked = cube[index]  96.1 us
    dot_general x54, matrix products, one_offset(): jnp.einsum('erc,erd->dc', picked, chosen, preferred_element_type=jnp.floa...  81.2 us
    dot_general x54, matrix products, convolve_add_offset(): jnp.einsum('erc,dc->erd', picked, kernel, preferred_element_type=jnp.floa...  74.3 us
    dot_general x54, matrix products, convolve_add_offset(): return (total + jnp.einsum('eb,erd->brd', choose, prod), None)  73.9 us
    dot_general x27, matrix products, spread_add_offset(): return (total + jnp.einsum('ex,erc->xrc', spot, contrib), None)  69.9 us
    gather x54, local copies, waits for them, and re-layouts, one_offset(): picked = cube[index]  59.5 us
    select_n x54, other arithmetic, one_offset(): picked = cube[index]  36.8 us
  transfers between devices with their start and end apart: 11, of which 7 were waited for; matrix products, arithmetic and copies ran while one was open for 49% of the time, Pallas kernels for 0%

commit v1 on v0

--- a/solution.py
+++ b/solution.py
@@ -43,7 +43,12 @@
     ).astype(jnp.float32)
 
     def widen(feat):
-        return lax.all_gather(feat, "chan", axis=1, tiled=True)
+        return jnp.concatenate(
+            lax.all_to_all(
+                jnp.stack([feat for _ in range(lax.axis_size("chan"))], axis=0), "chan", 0, 0
+            ),
+            axis=1,
+        )
 
     def attach_rims(feat):
         width = feat.shape[1]

time: 900 us -> 808 us (0.90)
  other arithmetic: 62.2 us -> 9.08 us
  local copies, waits for them, and re-layouts: 223 us -> 190 us
  matrix products: 331 us -> 307 us
  blocking collectives: 0 us -> 18.5 us
  waiting for transfers between devices: 240 us -> 230 us
    gather x54, local copies, waits for them, and re-layouts: 96.1 us -> 33.2 us  [convolve_add_offset(): picked = cube[index]]
    dot_general x54, matrix products: 73.9 us -> 31.2 us  [convolve_add_offset(): return (total + jnp.einsum('eb,erd->brd', choose, prod), None)]
    select_n x54, other arithmetic: 36.8 us -> 0.4 us  [one_offset(): picked = cube[index]]
    dot_general x54, matrix products: 81.2 us -> 114 us  [one_offset(): jnp.einsum('erc,erd->dc', picked, chosen, preferred_element_type=jnp.floa...]
    reduce_scatter x1, waiting for transfers between devices: 184 us -> 214 us  [local(): lax.psum_scatter(grad_one, 'space', scatter_dimension=2, tiled=True)]
    gather x54, local copies, waits for them, and re-layouts: 59.5 us -> 86 us  [one_offset(): picked = cube[index]]
    all_gather x2 -> x0, waiting for transfers between devices: 22.7 us -> none  [widen(): return lax.all_gather(feat, 'chan', axis=1, tiled=True)]
    unnamed x6 -> x4, waiting for transfers between devices: 22.1 us -> 0.07 us
  transfers between devices with their start and end apart: 11 -> 10, of which waited for: 7 -> 5; matrix products, arithmetic and copies ran while one was open for 49% -> 62% of each run, Pallas kernels for 0% -> 0%
where the time goes in v1:
time: 808 us; the launch traced here: 800 us
  matrix products  307 us (38%)
  waiting for transfers between devices  230 us (28%)
  local copies, waits for them, and re-layouts  190 us (24%)
  starting transfers between devices  22.9 us (3%)
  blocking collectives  18.5 us (2%)
  between operations  17.7 us (2%)
  other arithmetic  9.08 us (1%)
    reduce_scatter x1, waiting for transfers between devices, local(): lax.psum_scatter(grad_one, 'space', scatter_dimension=2, tiled=True)  214 us
    dot_general x54, matrix products, one_offset(): jnp.einsum('erc,erd->dc', picked, chosen, preferred_element_type=jnp.floa...  114 us
    gather x54, local copies, waits for them, and re-layouts, one_offset(): picked = cube[index]  86 us
    dot_general x27, matrix products, spread_add_offset(): return (total + jnp.einsum('ex,erc->xrc', spot, contrib), None)  69.8 us
    dot_general x54, matrix products, convolve_add_offset(): jnp.einsum('erc,dc->erd', picked, kernel, preferred_element_type=jnp.floa...  60.7 us
    convert_element_type x27, local copies, waits for them, and re-layouts, spread_add_offset(): chosen = jnp.einsum('eb,brd->erd', choose, grad_cube, preferred_element_t...  33.6 us
    gather x54, local copies, waits for them, and re-layouts, convolve_add_offset(): picked = cube[index]  33.2 us
    dot_general x54, matrix products, convolve_add_offset(): return (total + jnp.einsum('eb,erd->brd', choose, prod), None)  31.2 us
  transfers between devices with their start and end apart: 10, of which 5 were waited for; matrix products, arithmetic and copies ran while one was open for 62% of the time, Pallas kernels for 0%

profile of v1, /device:TPU:4, one launch (start us, length us, event | category | flops | bytes accessed | tf_op | source)
XLA Modules:
  0.0 799.6 jit_solution(11205785583324969650)
XLA Ops:
  10.1 6.4 all-to-all-start
  20.8 8.5 %all-to-all-done = bf16[8,2048,32]{1,2,0:T(8,128)(2,1)} async-done(((bf16[8,2048,32]{1,2,0:T(8,128)(2,1)}), bf16[8,2048,32]{1,2,0:T(8,128)(2,1)}, u32[]{:S(2)}, u32[]{:S(2)}) %all-to-all-start) | async-done | bytes 1048608 | tf_op jit(solution)/shard_map/all_to_all | solution.py:47
  31.7 2.9 collective-permute-start
  37.5 108.5 %while.58 = (s32[]{:T(128)}, f32[20,128,256]{2,0,1:T(8,128)S(1)}, bf16[27,16,20]{2,1,0:T(8,128)(2,1)}, bf16[27,16,16]{2,1,0:T(8,128)(2,1)S(1)}, bf16[16,128,32]{...) while((s32[]{:T(128)}, f32[20,128,256]{2,0,1:T(8,128)S(1)}, ...), condition=%wide.region_5.6_spmd.clone, body=%wide.region_4.5_spmd.clone.sunk | while | flops 57999360 | bytes 6317155 | solution.py:109
  38.9 2.6 select_add_fusion.2
  42.9 2.6 select_add_fusion.2
  46.9 2.6 select_add_fusion.2
  50.9 2.6 select_add_fusion.2
  55.0 2.6 select_add_fusion.2
  59.0 2.6 select_add_fusion.2
  63.0 2.6 select_add_fusion.2
  67.0 2.6 select_add_fusion.2
  71.0 2.6 select_add_fusion.2
  75.0 2.6 select_add_fusion.2
  79.1 2.6 select_add_fusion.2
  83.1 2.6 select_add_fusion.2
  87.1 2.6 select_add_fusion.2
  91.1 2.6 select_add_fusion.2
  95.1 2.6 select_add_fusion.2
  99.2 2.6 select_add_fusion.2
  103.2 2.6 select_add_fusion.2
  107.2 2.6 select_add_fusion.2
  111.2 2.6 select_add_fusion.2
  115.2 2.6 select_add_fusion.2
  119.3 2.6 select_add_fusion.2
  123.3 2.6 select_add_fusion.2
  127.3 2.6 select_add_fusion.2
  131.3 2.6 select_add_fusion.2
  135.3 2.6 select_add_fusion.2
  139.3 2.6 select_add_fusion.2
  143.4 2.6 select_add_fusion.2
  146.0 2.3 copy.61
  148.3 3.2 copy.67
  153.8 55.1 %while.56 = (s32[]{:T(128)}, f32[16,128,32]{1,0,2:T(8,128)S(1)}, bf16[27,16,16]{1,2,0:T(8,128)(2,1)S(1)}, s32[27,16]{1,0:T(8,128)S(1)}, bf16[20,128,256]{2,1,0:T...) while((s32[]{:T(128)}, f32[16,128,32]{1,0,2:T(8,128)S(1)}, ...), condition=%wide.region_1.2_spmd.clone, body=%wide.region_0.1_spmd.clone.sunk | while | flops 35783728 | bytes 3957607 | solution.py:75
  209.7 18.5 %all_to_all.10 = bf16[8,2048,32]{1,2,0:T(8,128)(2,1)S(1)} all-to-all(bf16[8,2048,32]{1,2,0:T(8,128)(2,1)S(1)} %stack.5), channel_id=1, replica_groups=mesh['space'=32,'chan'=8] {'chan'}, dimensions={0} | all-to-all | bytes 2097152 | tf_op jit(solution)/shard_map/all_to_all | solution.py:47
  228.7 4.5 collective-permute-start.2
  236.0 5.0 collective-permute-done.3
  246.0 5.1 collective-permute-start.4
  254.2 104.9 %while.55 = (s32[]{:T(128)}, f32[27,32,256]{2,1,0:T(8,128)}, bf16[27,16,16]{2,1,0:T(8,128)(2,1)S(1)}, bf16[16,128,32]{1,0,2:T(8,128)(2,1)S(1)}, s32[27,16]{1,0:T...) while((s32[]{:T(128)}, f32[27,32,256]{2,1,0:T(8,128)}, bf16[27,16,16]{2,1,0:T(8,128)(2,1)S(1)}, ...), condition=%wide.region_11.12_spmd, body=%wide.region_10.11_spmd.sunk | while | flops 35718192 | bytes 3580757 | solution.py:89
  359.0 3.3 copy.66
  365.6 2.3 copy.62
  375.3 123.3 %while.54 = (s32[]{:T(128)}, f32[27,32,256]{2,1,0:T(8,128)}, bf16[27,16,16]{2,1,0:T(8,128)(2,1)}, bf16[16,128,32]{1,0,2:T(8,128)(2,1)S(1)}, s32[27,16]{1,0:T(8,1...) while((s32[]{:T(128)}, f32[27,32,256]{2,1,0:T(8,128)}, bf16[27,16,16]{2,1,0:T(8,128)(2,1)}, ...), condition=%wide.region_8.9_spmd, body=%wide.region_7.8_spmd.sunk | while | flops 35718192 | bytes 3581265 | solution.py:89
  377.7 2.1 fusion.101
  405.1 2.1 fusion.101
  455.4 2.1 fusion.101
  498.6 3.3 copy.65
  502.0 73.4 %while.57 = (s32[]{:T(128)}, f32[16,128,32]{1,0,2:T(8,128)S(1)}, bf16[27,16,16]{1,2,0:T(8,128)(2,1)}, s32[27,16]{1,0:T(8,128)S(1)}, bf16[20,128,256]{2,1,0:T(8,1...) while((s32[]{:T(128)}, f32[16,128,32]{1,0,2:T(8,128)S(1)}, ...), condition=%wide.region_3.4_spmd.clone, body=%wide.region_2.3_spmd.clone.sunk | while | flops 35783728 | bytes 3958115 | solution.py:75
  578.1 214.0 %reduce-scatter.6.cloned.1.call-done = f32[27,32,8]{1,2,0:T(8,128)} async-done(((f32[27,32,256]{1,2,0:T(8,128)}), f32[27,32,8]{1,2,0:T(8,128)}) %reduce-scatter.6.cloned.1.call-update) | async-done | bytes 27664 | tf_op jit(solution)/shard_map/reduce_scatter | solution.py:127
  (660 shorter events, 422.3 us)
Async XLA Ops:
  8.0 8.5 %copy-start.3 = (s32[1,27,16,3]{1,2,3,0:T(8,128)S(1)}, s32[1,27,16,3]{1,2,3,0:T(8,128)}, u32[]{:S(2)}) copy-start(s32[1,27,16,3]{1,2,3,0:T(8,128)} %param.19) | copy-start | bytes 15556
  8.0 8.5 %copy-start.2 = (bf16[2048,32]{0,1:T(8,128)(2,1)S(1)}, bf16[2048,32]{0,1:T(8,128)(2,1)}, u32[]{:S(2)}) copy-start(bf16[2048,32]{0,1:T(8,128)(2,1)} %param.23) | copy-start | bytes 393220
  8.0 8.6 %copy-start.4 = (s32[32]{0:T(128)S(1)}, s32[32]{0:T(128)}, u32[]{:S(2)}) copy-start(s32[32]{0:T(128)} %param.20) | copy-start | bytes 388
  10.1 19.3 %all-to-all-start = ((bf16[8,2048,32]{1,2,0:T(8,128)(2,1)}), bf16[8,2048,32]{1,2,0:T(8,128)(2,1)}, u32[]{:S(2)}, u32[]{:S(2)}) async-start(bf16[8,2048,32]{1,2,0:T(8,128)(2,1)} %stack.4), calls=%async_computation | async-start | bytes 2097152 | tf_op jit(solution)/shard_map/all_to_all | solution.py:47
  16.5 227.3 %reduce-scatter.10.cloned.1.call-start = ((), (), s32[]{:S(2)}) async-start(), calls=%async_computation.7 | async-start | bytes 2949120
  31.7 120.1 %collective-permute-start = (bf16[256,256]{0,1:T(8,128)(2,1)}, bf16[256,256]{0,1:T(8,128)(2,1)}, u32[]{:S(2)}, u32[]{:S(2)}) collective-permute-start(bf16[256,256]{0,1:T(8,128)(2,1)} %bitcast.159), channel_id=1, source_target_pairs={{0,8},{8,16},{16,24},{24,32},{32,40},{40,48},{48,56},{56,64},{64,7... | collective-permute-start | bytes 393224 | tf_op jit(solution)/shard_map/ppermute | solution.py:17
  36.2 115.6 %collective-permute-start.1 = (bf16[256,256]{0,1:T(8,128)(2,1)}, bf16[256,256]{0,1:T(8,128)(2,1)}, u32[]{:S(2)}, u32[]{:S(2)}) collective-permute-start(bf16[256,256]{0,1:T(8,128)(2,1)} %bitcast.20), channel_id=1, source_target_pairs={{8,0},{16,8},{24,16},{32,24},{40,32},{48,40},{56,48},{64,56},{72,6... | collective-permute-start | bytes 393224 | tf_op jit(solution)/shard_map/ppermute | solution.py:18
  151.5 426.6 %reduce-scatter.8.cloned.1.call-start = ((), (), s32[]{:S(2)}) async-start(), calls=%async_computation.6 | async-start | bytes 3649536 | tf_op jit(solution)/shard_map/reduce_scatter | solution.py:128
  208.8 0.7 copy-start.1
  228.7 7.3 collective-permute-start.2
  233.9 7.1 collective-permute-start.3
  246.0 121.9 %collective-permute-start.4 = (f32[256,32]{1,0:T(8,128)}, f32[256,32]{1,0:T(8,128)}, u32[]{:S(2)}, u32[]{:S(2)}) collective-permute-start(f32[256,32]{1,0:T(8,128)} %copy.71), channel_id=1, source_target_pairs={{0,8},{8,16},{16,24},{24,32},{32,40},{40,48},{48,56},{56,64},{64,7... | collective-permute-start | bytes 98312 | tf_op jit(solution)/shard_map/ppermute | solution.py:17
  251.8 117.0 %collective-permute-start.5 = (f32[256,32]{1,0:T(8,128)}, f32[256,32]{1,0:T(8,128)}, u32[]{:S(2)}, u32[]{:S(2)}) collective-permute-start(f32[256,32]{1,0:T(8,128)} %copy.72), channel_id=1, source_target_pairs={{8,0},{16,8},{24,16},{32,24},{40,32},{48,40},{56,48},{64,56},{72,6... | collective-permute-start | bytes 98312 | tf_op jit(solution)/shard_map/ppermute | solution.py:18
  359.0 3.4 copy-start
  362.4 429.7 %reduce-scatter.6.cloned.1.call-start = ((), (), s32[]{:S(2)}) async-start(), calls=%async_computation.5 | async-start | bytes 3649536 | tf_op jit(solution)/shard_map/reduce_scatter | solution.py:127
Sparse Core Ops, SparseCore 0:
  151.7 37.3 reduce-scatter.9
Sparse Core Ops, SparseCore 1:
  362.5 215.5 reduce-scatter.7
  583.0 209.1 reduce-scatter.5
